TPU v7x, 32 devices: a whole 2x2x4 slice. The times are simulated.
32 devices in a mesh: case: 2 (over y), blk: 4 (over z), freq: 4 (over x, core).
Axes of the slice: x: 2, y: 2, z: 4, core: 2. Of those that a mesh axis runs over, the one named last changes fastest.
Arguments:
- geometry: bfloat16 [3, 8192], P(None, ('case', 'blk')), parts along dimension 1, may hold values from -4 to 4
- modes: bfloat16 [4, 8192, 128], P('freq', ('case', 'blk')), parts along dimension 1, may hold values from -6 to 6
- reduced_freq: float32 [16], replicated, may hold values from 0.1 to 1.5
- freq_index: int32 [8, 3], P(('case', 'freq')), parts along dimension 0, may hold values from 0 to 15
Outputs:
- grad_geometry: float32 [3, 8192], P(None, ('case', 'blk', 'freq')), parts along dimension 1
- forces: float32 [8, 2, 32, 32], P(('case', 'freq')), parts along dimension 0
There are 2 independent parts, one for each index of `case`. A program takes and returns all parts, laid end to end along the dimension named above; an argument that names none is the same for every part. Nothing has to cross between parts.
All inputs are finite; a program needn't handle non-finite values.
Results may differ from a plain program's by a relative error of at most 0.003.
Values may be sent and summed in bfloat16 or wider, within the bound.
No kernel may reach another device: no remote copies, remote signals or barrier semaphores. Data moves between devices by JAX's collectives and lax.ppermute only.
A program may use at most 64 MiB of HBM per device.

v0:
```python
import math
import jax
import jax.numpy as jnp
from jax import lax
from jax.sharding import PartitionSpec as P

CHORD_SHIFT = 0.5
CORE_SQUARE = 0.25


def passed_along(value, axis, steps):
    count = lax.axis_size(axis)
    pairs = [(source, (source + steps) % count) for source in range(count)]
    return lax.ppermute(value, axis, pairs)


def prepare_sender(send_modes):
    columns = send_modes.shape[1] // 4
    flipped = jnp.concatenate([send_modes[:, 2 * columns :], send_modes[:, : 2 * columns]], axis=1)
    turned = jnp.concatenate(
        [
            send_modes[:, 3 * columns :],
            -send_modes[:, 2 * columns : 3 * columns],
            send_modes[:, columns : 2 * columns],
            -send_modes[:, :columns],
        ],
        axis=1,
    )
    paired = jnp.concatenate([flipped, turned], axis=0)
    strength = jnp.concatenate(
        [
            send_modes[:, 2 * columns :],
            jnp.concatenate(
                [-send_modes[:, 3 * columns :], send_modes[:, 2 * columns : 3 * columns]], axis=1
            ),
        ],
        axis=0,
    )
    return (paired, strength)


def block_terms(recv_geom, recv_modes, send_pos, paired, strength, wavenumber):
    send_count = send_pos.shape[1]
    coupled = lax.dot_general(
        recv_modes, paired, (((1,), (1,)), ((), ())), preferred_element_type=jnp.float32
    )
    real_part = coupled[:, :send_count]
    imag_part = coupled[:, send_count:]
    recv_pos = recv_geom.astype(jnp.float32)
    delta_x = recv_pos[0][:, None] + CHORD_SHIFT - send_pos[0][None, :]
    delta_y = recv_pos[1][:, None] - send_pos[1][None, :]
    delta_z = recv_pos[2][:, None] - send_pos[2][None, :]
    inverse = lax.rsqrt(delta_x * delta_x + delta_y * delta_y + delta_z * delta_z + CORE_SQUARE)
    phase = wavenumber * delta_x
    cosine = jnp.cos(phase)
    sine = jnp.sin(phase)
    along = cosine * real_part + sine * imag_part
    across = cosine * imag_part - sine * real_part
    cubed = inverse * inverse * inverse * along
    grad_x = wavenumber * inverse * across - delta_x * cubed
    grad_y = -delta_y * cubed
    grad_z = -delta_z * cubed
    row_grad = jnp.stack([grad_x.sum(axis=1), grad_y.sum(axis=1), grad_z.sum(axis=1)])
    col_grad = -jnp.stack([grad_x.sum(axis=0), grad_y.sum(axis=0), grad_z.sum(axis=0)])
    kernel = jnp.concatenate([cosine * inverse, -sine * inverse], axis=1).astype(jnp.bfloat16)
    pressure = jnp.dot(kernel, strength, preferred_element_type=jnp.float32)
    return (row_grad, col_grad, pressure)


def spread(stacked):
    return lax.psum_scatter(stacked, "freq", scatter_dimension=2, tiled=True)


def local(geometry, modes, reduced_freq, freq_index):
    row_count = geometry.shape[1]
    own_modes = modes[0]
    columns = own_modes.shape[1] // 4
    steps = freq_index.shape[1]
    table_size = reduced_freq.shape[0]
    selected = freq_index[0][:, None] == jnp.arange(table_size, dtype=jnp.int32)[None, :]
    wavenumbers = jnp.sum(jnp.where(selected, reduced_freq[None, :], 0.0), axis=1)
    local_block = (geometry, own_modes)
    sending = [local_block]
    current = local_block
    for offset in range(1, steps):
        current = passed_along((current[0], current[1]), "blk", 1)
        sending.append(current)
    block_rows = min(128, row_count)
    block_count = row_count // block_rows
    recv_geom = geometry.reshape(3, block_count, block_rows).transpose(1, 0, 2)
    recv_modes = own_modes.reshape(block_count, block_rows, 4 * columns)
    row_total = jnp.zeros((3, row_count), jnp.float32)
    pressure_total = jnp.zeros((row_count, 2 * columns), jnp.float32)
    col_parts = []
    for offset in range(steps):
        send_geom, send_modes = sending[offset]
        paired, strength = prepare_sender(send_modes)
        send_pos = send_geom.astype(jnp.float32)
        wavenumber = wavenumbers[offset]

        def visit(
            carry,
            operands,
            send_pos=send_pos,
            paired=paired,
            strength=strength,
            wavenumber=wavenumber,
        ):
            row_grad, col_grad, pressure = block_terms(
                operands[0], operands[1], send_pos, paired, strength, wavenumber
            )
            return (carry + col_grad, (row_grad, pressure))

        col_grad, (row_parts, pressure_parts) = lax.scan(
            visit, jnp.zeros((3, row_count), jnp.float32), (recv_geom, recv_modes)
        )
        row_total = row_total + row_parts.transpose(1, 0, 2).reshape(3, row_count)
        pressure_total = pressure_total + pressure_parts.reshape(row_count, 2 * columns)
        col_parts.append(col_grad)
    local_grad = row_total + col_parts[0]
    grad_scale = 1.0 / math.sqrt(columns * steps * row_count * lax.axis_size("freq"))
    total = local_grad
    for offset in range(1, steps):
        total = total + passed_along(col_parts[offset], "blk", -offset)
    result = spread((total * grad_scale)[None])[0]
    adjoint = own_modes[:, : 2 * columns].astype(jnp.float32)
    adj_real = adjoint[:, :columns]
    adj_imag = adjoint[:, columns:]
    press_real = pressure_total[:, :columns]
    press_imag = pressure_total[:, columns:]
    contract = (((0,), (0,)), ((), ()))
    force_real = lax.dot_general(
        adj_real, press_real, contract, precision=lax.Precision.HIGHEST
    ) + lax.dot_general(adj_imag, press_imag, contract, precision=lax.Precision.HIGHEST)
    force_imag = lax.dot_general(
        adj_real, press_imag, contract, precision=lax.Precision.HIGHEST
    ) - lax.dot_general(adj_imag, press_real, contract, precision=lax.Precision.HIGHEST)
    force_local = jnp.stack([force_real, force_imag])
    force_total = lax.psum(force_local, "blk")
    force_scale = 1.0 / math.sqrt(row_count * row_count * lax.axis_size("blk") * steps)
    return (result, (force_total * force_scale)[None])


def solution(mesh):
    return jax.shard_map(
        local,
        mesh=mesh,
        in_specs=(
            P(None, ("case", "blk")),
            P("freq", ("case", "blk"), None),
            P(),
            P(("case", "freq"), None),
        ),
        out_specs=(P(None, ("case", "blk", "freq")), P(("case", "freq"), None, None, None)),
        check_vma=False,
    )
```

profile of v0, /device:TPU:0, one launch (start us, length us, event | category | flops | bytes accessed | tf_op | source)
XLA Modules:
  0.0 178.1 jit_solution(9225079058068563746)
XLA Ops:
  19.0 34.4 %while.45 = (s32[]{:T(128)}, f32[3,1024]{1,0:T(4,128)S(1)}, f32[8,3,128]{2,1,0:T(4,128)S(1)}, f32[8,128,64]{1,2,0:T(8,128)S(1)}, f32[]{:T(128)}, /*index=5*/bf16...) while((s32[]{:T(128)}, f32[3,1024]{1,0:T(4,128)S(1)}, ...), condition=%wide.region_8.9_spmd.clone, body=%wide.region_1.8_spmd.clone.sunk | while | flops 106967936 | bytes 6464403 | solution.py:114
  19.4 3.2 %fusion.185 = (bf16[128,1024]{1,0:T(8,128)(2,1)S(1)}, bf16[128,1024]{1,0:T(8,128)(2,1)S(1)}, f32[128,1024]{1,0:T(8,128)S(1)}, f32[128,1024]{1,0:T(8,128)S(1)}) fusion(f32[1024]{0:T(1024)S(1)} %bitcast.228, f32[128]{0:T(128)S(1)} %get-tuple-element.645, f32[1024]{0:T(1024)S(1)} %bitcast.230, f32[128]{0:T(128)S(1)} %get-tuple-element.647, ...), kind=kLoop, calls=%fused_computation.25.clone.1 | loop fusion | flops 3670016 | bytes 2635268 | tf_op jit(solution)/shard_map/convert
  23.7 3.2 %fusion.185 = (bf16[128,1024]{1,0:T(8,128)(2,1)S(1)}, bf16[128,1024]{1,0:T(8,128)(2,1)S(1)}, f32[128,1024]{1,0:T(8,128)S(1)}, f32[128,1024]{1,0:T(8,128)S(1)}) fusion(f32[1024]{0:T(1024)S(1)} %bitcast.228, f32[128]{0:T(128)S(1)} %get-tuple-element.645, f32[1024]{0:T(1024)S(1)} %bitcast.230, f32[128]{0:T(128)S(1)} %get-tuple-element.647, ...), kind=kLoop, calls=%fused_computation.25.clone.1 | loop fusion | flops 3670016 | bytes 2635268 | tf_op jit(solution)/shard_map/convert
  28.0 3.2 %fusion.185 = (bf16[128,1024]{1,0:T(8,128)(2,1)S(1)}, bf16[128,1024]{1,0:T(8,128)(2,1)S(1)}, f32[128,1024]{1,0:T(8,128)S(1)}, f32[128,1024]{1,0:T(8,128)S(1)}) fusion(f32[1024]{0:T(1024)S(1)} %bitcast.228, f32[128]{0:T(128)S(1)} %get-tuple-element.645, f32[1024]{0:T(1024)S(1)} %bitcast.230, f32[128]{0:T(128)S(1)} %get-tuple-element.647, ...), kind=kLoop, calls=%fused_computation.25.clone.1 | loop fusion | flops 3670016 | bytes 2635268 | tf_op jit(solution)/shard_map/convert
  32.3 3.2 %fusion.185 = (bf16[128,1024]{1,0:T(8,128)(2,1)S(1)}, bf16[128,1024]{1,0:T(8,128)(2,1)S(1)}, f32[128,1024]{1,0:T(8,128)S(1)}, f32[128,1024]{1,0:T(8,128)S(1)}) fusion(f32[1024]{0:T(1024)S(1)} %bitcast.228, f32[128]{0:T(128)S(1)} %get-tuple-element.645, f32[1024]{0:T(1024)S(1)} %bitcast.230, f32[128]{0:T(128)S(1)} %get-tuple-element.647, ...), kind=kLoop, calls=%fused_computation.25.clone.1 | loop fusion | flops 3670016 | bytes 2635268 | tf_op jit(solution)/shard_map/convert
  36.6 3.2 %fusion.185 = (bf16[128,1024]{1,0:T(8,128)(2,1)S(1)}, bf16[128,1024]{1,0:T(8,128)(2,1)S(1)}, f32[128,1024]{1,0:T(8,128)S(1)}, f32[128,1024]{1,0:T(8,128)S(1)}) fusion(f32[1024]{0:T(1024)S(1)} %bitcast.228, f32[128]{0:T(128)S(1)} %get-tuple-element.645, f32[1024]{0:T(1024)S(1)} %bitcast.230, f32[128]{0:T(128)S(1)} %get-tuple-element.647, ...), kind=kLoop, calls=%fused_computation.25.clone.1 | loop fusion | flops 3670016 | bytes 2635268 | tf_op jit(solution)/shard_map/convert
  40.9 3.2 %fusion.185 = (bf16[128,1024]{1,0:T(8,128)(2,1)S(1)}, bf16[128,1024]{1,0:T(8,128)(2,1)S(1)}, f32[128,1024]{1,0:T(8,128)S(1)}, f32[128,1024]{1,0:T(8,128)S(1)}) fusion(f32[1024]{0:T(1024)S(1)} %bitcast.228, f32[128]{0:T(128)S(1)} %get-tuple-element.645, f32[1024]{0:T(1024)S(1)} %bitcast.230, f32[128]{0:T(128)S(1)} %get-tuple-element.647, ...), kind=kLoop, calls=%fused_computation.25.clone.1 | loop fusion | flops 3670016 | bytes 2635268 | tf_op jit(solution)/shard_map/convert
  45.2 3.2 %fusion.185 = (bf16[128,1024]{1,0:T(8,128)(2,1)S(1)}, bf16[128,1024]{1,0:T(8,128)(2,1)S(1)}, f32[128,1024]{1,0:T(8,128)S(1)}, f32[128,1024]{1,0:T(8,128)S(1)}) fusion(f32[1024]{0:T(1024)S(1)} %bitcast.228, f32[128]{0:T(128)S(1)} %get-tuple-element.645, f32[1024]{0:T(1024)S(1)} %bitcast.230, f32[128]{0:T(128)S(1)} %get-tuple-element.647, ...), kind=kLoop, calls=%fused_computation.25.clone.1 | loop fusion | flops 3670016 | bytes 2635268 | tf_op jit(solution)/shard_map/convert
  49.5 3.2 %fusion.185 = (bf16[128,1024]{1,0:T(8,128)(2,1)S(1)}, bf16[128,1024]{1,0:T(8,128)(2,1)S(1)}, f32[128,1024]{1,0:T(8,128)S(1)}, f32[128,1024]{1,0:T(8,128)S(1)}) fusion(f32[1024]{0:T(1024)S(1)} %bitcast.228, f32[128]{0:T(128)S(1)} %get-tuple-element.645, f32[1024]{0:T(1024)S(1)} %bitcast.230, f32[128]{0:T(128)S(1)} %get-tuple-element.647, ...), kind=kLoop, calls=%fused_computation.25.clone.1 | loop fusion | flops 3670016 | bytes 2635268 | tf_op jit(solution)/shard_map/convert
  56.0 34.7 %while.46 = (s32[]{:T(128)}, f32[3,1024]{1,0:T(4,128)S(1)}, f32[8,3,128]{2,1,0:T(4,128)S(1)}, f32[8,128,64]{1,2,0:T(8,128)S(1)}, f32[]{:T(128)}, /*index=5*/bf16...) while((s32[]{:T(128)}, f32[3,1024]{1,0:T(4,128)S(1)}, ...), condition=%wide.region_16.17_spmd.clone, body=%wide.region_9.16_spmd.clone.sunk | while | flops 106967936 | bytes 6464403 | solution.py:114
  56.4 3.2 %fusion.196 = (bf16[128,1024]{1,0:T(8,128)(2,1)S(1)}, bf16[128,1024]{1,0:T(8,128)(2,1)S(1)}, f32[128,1024]{1,0:T(8,128)S(1)}, f32[128,1024]{1,0:T(8,128)S(1)}) fusion(f32[1024]{0:T(1024)S(1)} %bitcast.232, f32[128]{0:T(128)S(1)} %get-tuple-element.671, f32[1024]{0:T(1024)S(1)} %bitcast.234, f32[128]{0:T(128)S(1)} %get-tuple-element.673, ...), kind=kLoop, calls=%fused_computation.77.clone.1 | loop fusion | flops 3670016 | bytes 2635268 | tf_op jit(solution)/shard_map/convert.2
  60.8 3.2 %fusion.196 = (bf16[128,1024]{1,0:T(8,128)(2,1)S(1)}, bf16[128,1024]{1,0:T(8,128)(2,1)S(1)}, f32[128,1024]{1,0:T(8,128)S(1)}, f32[128,1024]{1,0:T(8,128)S(1)}) fusion(f32[1024]{0:T(1024)S(1)} %bitcast.232, f32[128]{0:T(128)S(1)} %get-tuple-element.671, f32[1024]{0:T(1024)S(1)} %bitcast.234, f32[128]{0:T(128)S(1)} %get-tuple-element.673, ...), kind=kLoop, calls=%fused_computation.77.clone.1 | loop fusion | flops 3670016 | bytes 2635268 | tf_op jit(solution)/shard_map/convert.2
  65.1 3.2 %fusion.196 = (bf16[128,1024]{1,0:T(8,128)(2,1)S(1)}, bf16[128,1024]{1,0:T(8,128)(2,1)S(1)}, f32[128,1024]{1,0:T(8,128)S(1)}, f32[128,1024]{1,0:T(8,128)S(1)}) fusion(f32[1024]{0:T(1024)S(1)} %bitcast.232, f32[128]{0:T(128)S(1)} %get-tuple-element.671, f32[1024]{0:T(1024)S(1)} %bitcast.234, f32[128]{0:T(128)S(1)} %get-tuple-element.673, ...), kind=kLoop, calls=%fused_computation.77.clone.1 | loop fusion | flops 3670016 | bytes 2635268 | tf_op jit(solution)/shard_map/convert.2
  69.4 3.2 %fusion.196 = (bf16[128,1024]{1,0:T(8,128)(2,1)S(1)}, bf16[128,1024]{1,0:T(8,128)(2,1)S(1)}, f32[128,1024]{1,0:T(8,128)S(1)}, f32[128,1024]{1,0:T(8,128)S(1)}) fusion(f32[1024]{0:T(1024)S(1)} %bitcast.232, f32[128]{0:T(128)S(1)} %get-tuple-element.671, f32[1024]{0:T(1024)S(1)} %bitcast.234, f32[128]{0:T(128)S(1)} %get-tuple-element.673, ...), kind=kLoop, calls=%fused_computation.77.clone.1 | loop fusion | flops 3670016 | bytes 2635268 | tf_op jit(solution)/shard_map/convert.2
  73.8 3.2 %fusion.196 = (bf16[128,1024]{1,0:T(8,128)(2,1)S(1)}, bf16[128,1024]{1,0:T(8,128)(2,1)S(1)}, f32[128,1024]{1,0:T(8,128)S(1)}, f32[128,1024]{1,0:T(8,128)S(1)}) fusion(f32[1024]{0:T(1024)S(1)} %bitcast.232, f32[128]{0:T(128)S(1)} %get-tuple-element.671, f32[1024]{0:T(1024)S(1)} %bitcast.234, f32[128]{0:T(128)S(1)} %get-tuple-element.673, ...), kind=kLoop, calls=%fused_computation.77.clone.1 | loop fusion | flops 3670016 | bytes 2635268 | tf_op jit(solution)/shard_map/convert.2
  78.1 3.2 %fusion.196 = (bf16[128,1024]{1,0:T(8,128)(2,1)S(1)}, bf16[128,1024]{1,0:T(8,128)(2,1)S(1)}, f32[128,1024]{1,0:T(8,128)S(1)}, f32[128,1024]{1,0:T(8,128)S(1)}) fusion(f32[1024]{0:T(1024)S(1)} %bitcast.232, f32[128]{0:T(128)S(1)} %get-tuple-element.671, f32[1024]{0:T(1024)S(1)} %bitcast.234, f32[128]{0:T(128)S(1)} %get-tuple-element.673, ...), kind=kLoop, calls=%fused_computation.77.clone.1 | loop fusion | flops 3670016 | bytes 2635268 | tf_op jit(solution)/shard_map/convert.2
  82.5 3.2 %fusion.196 = (bf16[128,1024]{1,0:T(8,128)(2,1)S(1)}, bf16[128,1024]{1,0:T(8,128)(2,1)S(1)}, f32[128,1024]{1,0:T(8,128)S(1)}, f32[128,1024]{1,0:T(8,128)S(1)}) fusion(f32[1024]{0:T(1024)S(1)} %bitcast.232, f32[128]{0:T(128)S(1)} %get-tuple-element.671, f32[1024]{0:T(1024)S(1)} %bitcast.234, f32[128]{0:T(128)S(1)} %get-tuple-element.673, ...), kind=kLoop, calls=%fused_computation.77.clone.1 | loop fusion | flops 3670016 | bytes 2635268 | tf_op jit(solution)/shard_map/convert.2
  86.8 3.2 %fusion.196 = (bf16[128,1024]{1,0:T(8,128)(2,1)S(1)}, bf16[128,1024]{1,0:T(8,128)(2,1)S(1)}, f32[128,1024]{1,0:T(8,128)S(1)}, f32[128,1024]{1,0:T(8,128)S(1)}) fusion(f32[1024]{0:T(1024)S(1)} %bitcast.232, f32[128]{0:T(128)S(1)} %get-tuple-element.671, f32[1024]{0:T(1024)S(1)} %bitcast.234, f32[128]{0:T(128)S(1)} %get-tuple-element.673, ...), kind=kLoop, calls=%fused_computation.77.clone.1 | loop fusion | flops 3670016 | bytes 2635268 | tf_op jit(solution)/shard_map/convert.2
  94.6 34.4 %while.47 = (s32[]{:T(128)}, f32[3,1024]{1,0:T(4,128)S(1)}, f32[8,3,128]{2,1,0:T(4,128)S(1)}, f32[8,128,64]{1,2,0:T(8,128)S(1)}, f32[]{:T(128)}, /*index=5*/bf16...) while((s32[]{:T(128)}, f32[3,1024]{1,0:T(4,128)S(1)}, ...), condition=%wide.region_24.25_spmd.clone, body=%wide.region_17.24_spmd.clone.sunk | while | flops 106967936 | bytes 6464403 | solution.py:114
  94.9 3.2 %fusion.207 = (bf16[128,1024]{1,0:T(8,128)(2,1)S(1)}, bf16[128,1024]{1,0:T(8,128)(2,1)S(1)}, f32[128,1024]{1,0:T(8,128)S(1)}, f32[128,1024]{1,0:T(8,128)S(1)}) fusion(f32[1024]{0:T(1024)S(1)} %bitcast.236, f32[128]{0:T(128)S(1)} %get-tuple-element.697, f32[1024]{0:T(1024)S(1)} %bitcast.238, f32[128]{0:T(128)S(1)} %get-tuple-element.699, ...), kind=kLoop, calls=%fused_computation.129.clone.1 | loop fusion | flops 3670016 | bytes 2635268 | tf_op jit(solution)/shard_map/convert.4
  99.2 3.2 %fusion.207 = (bf16[128,1024]{1,0:T(8,128)(2,1)S(1)}, bf16[128,1024]{1,0:T(8,128)(2,1)S(1)}, f32[128,1024]{1,0:T(8,128)S(1)}, f32[128,1024]{1,0:T(8,128)S(1)}) fusion(f32[1024]{0:T(1024)S(1)} %bitcast.236, f32[128]{0:T(128)S(1)} %get-tuple-element.697, f32[1024]{0:T(1024)S(1)} %bitcast.238, f32[128]{0:T(128)S(1)} %get-tuple-element.699, ...), kind=kLoop, calls=%fused_computation.129.clone.1 | loop fusion | flops 3670016 | bytes 2635268 | tf_op jit(solution)/shard_map/convert.4
  112.2 3.2 %fusion.207 = (bf16[128,1024]{1,0:T(8,128)(2,1)S(1)}, bf16[128,1024]{1,0:T(8,128)(2,1)S(1)}, f32[128,1024]{1,0:T(8,128)S(1)}, f32[128,1024]{1,0:T(8,128)S(1)}) fusion(f32[1024]{0:T(1024)S(1)} %bitcast.236, f32[128]{0:T(128)S(1)} %get-tuple-element.697, f32[1024]{0:T(1024)S(1)} %bitcast.238, f32[128]{0:T(128)S(1)} %get-tuple-element.699, ...), kind=kLoop, calls=%fused_computation.129.clone.1 | loop fusion | flops 3670016 | bytes 2635268 | tf_op jit(solution)/shard_map/convert.4
  130.8 17.7 %psum.7 = f32[2,32,32]{1,2,0:T(8,128)S(1)} all-reduce(f32[2,32,32]{1,2,0:T(8,128)S(1)} %pad_maximum_fusion), channel_id=1, replica_groups=mesh['case'=2,'blk'=4,'freq'=4] {'blk'}, use_global_device_ids=true, to_apply=%region_26.27 | all-reduce | flops 2048 | bytes 16384 | tf_op jit(solution)/shard_map/psum | solution.py:139
  150.4 19.2 %reduce-scatter.4.cloned.1.call-done = f32[256,3]{1,0:T(8,128)} async-done(((f32[1024,3]{1,0:T(8,128)}), f32[256,3]{1,0:T(8,128)}) %reduce-scatter.4.cloned.1.call-update) | async-done | bytes 3088
  (256 shorter events, 64.9 us)
Async XLA Ops:
  7.2 162.5 %reduce-scatter.4.cloned.1.call-start = ((), (), s32[]{:S(2)}) async-start(), calls=%async_computation.1 | async-start | bytes 655360
  7.2 46.3 %collective-permute-start.1 = (bf16[1024,128]{1,0:T(8,128)(2,1)}, bf16[1024,128]{1,0:T(8,128)(2,1)S(1)}, u32[]{:S(2)}, u32[]{:S(2)}) collective-permute-start(bf16[1024,128]{1,0:T(8,128)(2,1)} %bitcast.219), channel_id=1, source_target_pairs={{0,4},{4,8},{8,12},{12,0},{1,5},{5,9},{9,13},{13,1},{2,6},{6,10},{... | collective-permute-start | bytes 786440 | tf_op jit(solution)/shard_map/ppermute | solution.py:14
  10.3 8.7 %collective-permute-start = (bf16[3,1024]{1,0:T(4,128)(2,1)}, bf16[3,1024]{1,0:T(4,128)(2,1)S(1)}, u32[]{:S(2)}, u32[]{:S(2)}) collective-permute-start(bf16[3,1024]{1,0:T(4,128)(2,1)} %param.10), channel_id=1, source_target_pairs={{0,4},{4,8},{8,12},{12,0},{1,5},{5,9},{9,13},{13,1},{2,6},{6,10},{... | collective-permute-start | bytes 18440 | tf_op jit(solution)/shard_map/ppermute | solution.py:14
  11.9 1.7 copy-start
  13.7 0.7 copy-start.2
  13.7 0.7 copy-start.3
  14.8 1.2 copy-start.1
  19.0 34.5 %collective-permute-start.2 = (bf16[3,1024]{1,0:T(4,128)(2,1)S(1)}, bf16[3,1024]{1,0:T(4,128)(2,1)S(1)}, u32[]{:S(2)}, u32[]{:S(2)}) collective-permute-start(bf16[3,1024]{1,0:T(4,128)(2,1)S(1)} %collective-permute-done), channel_id=1, source_target_pairs={{0,4},{4,8},{8,12},{12,0},{1,5},{5,9},{9,13},{13,1},{2,6},{6,10},{... | collective-permute-start | bytes 18440 | tf_op jit(solution)/shard_map/ppermute | solution.py:14
  54.7 38.7 %collective-permute-start.3 = (bf16[1024,128]{1,0:T(8,128)(2,1)S(1)}, bf16[1024,128]{1,0:T(8,128)(2,1)S(1)}, u32[]{:S(2)}, u32[]{:S(2)}) collective-permute-start(bf16[1024,128]{1,0:T(8,128)(2,1)S(1)} %collective-permute-done.1), channel_id=1, source_target_pairs={{0,4},{4,8},{8,12},{12,0},{1,5},{5,9},{9,13},{13,1},{2,6},{6,10},{... | collective-permute-start | bytes 786440 | tf_op jit(solution)/shard_map/ppermute | solution.py:14
  90.8 57.8 %collective-permute-start.4 = (f32[3,1024]{1,0:T(4,128)S(1)}, f32[3,1024]{1,0:T(4,128)S(1)}, u32[]{:S(2)}, u32[]{:S(2)}) collective-permute-start(f32[3,1024]{1,0:T(4,128)S(1)} %get-tuple-element.168), channel_id=1, source_target_pairs={{0,12},{4,0},{8,4},{12,8},{1,13},{5,1},{9,5},{13,9},{2,14},{6,2},{... | collective-permute-start | bytes 36872 | tf_op jit(solution)/shard_map/ppermute | solution.py:14
  130.2 18.4 %collective-permute-start.5 = (f32[3,1024]{1,0:T(4,128)S(1)}, f32[3,1024]{1,0:T(4,128)S(1)}, u32[]{:S(2)}, u32[]{:S(2)}) collective-permute-start(f32[3,1024]{1,0:T(4,128)S(1)} %get-tuple-element.169), channel_id=1, source_target_pairs={{0,8},{4,12},{8,0},{12,4},{1,9},{5,13},{9,1},{13,5},{2,10},{6,14},... | collective-permute-start | bytes 36872 | tf_op jit(solution)/shard_map/ppermute | solution.py:14
Sparse Core Ops, SparseCore 0:
  149.8 19.7 reduce-scatter.3
where the time goes:
time: 178 us
  other arithmetic  91.4 us (51%)
  waiting for transfers between devices  22.3 us (13%)
  blocking collectives  17.7 us (10%)
  matrix products  16.2 us (9%)
  between operations  14.3 us (8%)
  starting transfers between devices  9.26 us (5%)
  local copies, waits for them, and re-layouts  5.38 us (3%)
    another operation x24, other arithmetic  76.2 us
    unnamed x2, waiting for transfers between devices  19.3 us
    psum x1, blocking collectives, local(): force_total = lax.psum(force_local, 'blk')  17.7 us
    ppermute x6, starting transfers between devices, passed_along(): return lax.ppermute(value, axis, pairs)  9.23 us
    reduce_sum x24, other arithmetic, block_terms(): grad_y.sum(axis=1)  9.08 us
    dot_general x24, matrix products, block_terms(): pressure = jnp.dot(kernel, strength, preferred_element_type=jnp.float32)  7.89 us
    dot_general x24, matrix products, block_terms(): lax.dot_general(recv_modes, paired, (((1,), (1,)), ((), ())), preferred_e...  7.17 us
    unnamed x11, local copies, waits for them, and re-layouts  3.97 us
  transfers between devices with their start and end apart: 7, of which 2 were waited for; matrix products, arithmetic and copies ran while one was open for 61% of the time, Pallas kernels for 0%

commit v1 on v0

--- a/solution.py
+++ b/solution.py
@@ -1,11 +1,26 @@
+import functools
 import math
 import jax
 import jax.numpy as jnp
 from jax import lax
 from jax.sharding import PartitionSpec as P
+from jax.lax import axis_size, ppermute
 
 CHORD_SHIFT = 0.5
 CORE_SQUARE = 0.25
+
+
+def arrays_find(inner_x, mesh_dim):
+    nodes = axis_size(mesh_dim)
+    back = lambda v1: [(it, it ^ v1) for it in range(nodes)]
+    newest = inner_x
+    for i0 in range(nodes.bit_length() - 1):
+        local_part = ppermute(newest, mesh_dim, back(1 << i0))
+        newest = newest + local_part
+    return newest
+
+
+map_handle = functools.partial(arrays_find, mesh_dim="blk")
 
 
 def passed_along(value, axis, steps):
@@ -136,7 +151,7 @@
         adj_real, press_imag, contract, precision=lax.Precision.HIGHEST
     ) - lax.dot_general(adj_imag, press_real, contract, precision=lax.Precision.HIGHEST)
     force_local = jnp.stack([force_real, force_imag])
-    force_total = lax.psum(force_local, "blk")
+    force_total = map_handle(force_local)
     force_scale = 1.0 / math.sqrt(row_count * row_count * lax.axis_size("blk") * steps)
     return (result, (force_total * force_scale)[None])
 

time: 178 us -> 167 us (0.938)
  blocking collectives: 17.7 us -> 0 us
  starting transfers between devices: 9.26 us -> 13.7 us
  waiting for transfers between devices: 22.3 us -> 24.3 us
    psum x1 -> x0, blocking collectives: 17.7 us -> none  [local(): force_total = lax.psum(force_local, 'blk')]
    ppermute x0 -> x2, starting transfers between devices: none -> 4.64 us  [arrays_find(): local_part = ppermute(newest, mesh_dim, back(1 << i0))]
  transfers between devices with their start and end apart: 7 -> 9, of which waited for: 2 -> 3; matrix products, arithmetic and copies ran while one was open for 61% -> 44% of each run, Pallas kernels for 0% -> 0%
where the time goes in v1:
time: 167 us
  other arithmetic  91.5 us (55%)
  waiting for transfers between devices  24.3 us (15%)
  matrix products  16.2 us (10%)
  between operations  14.3 us (9%)
  starting transfers between devices  13.7 us (8%)
  local copies, waits for them, and re-layouts  5.38 us (3%)
    another operation x24, other arithmetic  76.2 us
    unnamed x2, waiting for transfers between devices  19.7 us
    reduce_sum x24, other arithmetic, block_terms(): grad_y.sum(axis=1)  9.08 us
    ppermute x6, starting transfers between devices, passed_along(): return lax.ppermute(value, axis, pairs)  8.97 us
    dot_general x24, matrix products, block_terms(): pressure = jnp.dot(kernel, strength, preferred_element_type=jnp.float32)  7.89 us
    dot_general x24, matrix products, block_terms(): lax.dot_general(recv_modes, paired, (((1,), (1,)), ((), ())), preferred_e...  7.17 us
    ppermute x6, waiting for transfers between devices, passed_along(): return lax.ppermute(value, axis, pairs)  4.66 us
    ppermute x2, starting transfers between devices, arrays_find(): local_part = ppermute(newest, mesh_dim, back(1 << i0))  4.64 us
  transfers between devices with their start and end apart: 9, of which 3 were waited for; matrix products, arithmetic and copies ran while one was open for 44% of the time, Pallas kernels for 0%

profile of v1, /device:TPU:0, one launch (start us, length us, event | category | flops | bytes accessed | tf_op | source)
XLA Modules:
  0.0 166.8 jit_solution(8865427343421972517)
XLA Ops:
  19.0 34.4 %while.45 = (s32[]{:T(128)}, f32[3,1024]{1,0:T(4,128)S(1)}, f32[8,3,128]{2,1,0:T(4,128)S(1)}, f32[8,128,64]{1,2,0:T(8,128)S(1)}, f32[]{:T(128)}, /*index=5*/bf16...) while((s32[]{:T(128)}, f32[3,1024]{1,0:T(4,128)S(1)}, ...), condition=%wide.region_8.9_spmd.clone, body=%wide.region_1.8_spmd.clone.sunk | while | flops 106967936 | bytes 6464403 | solution.py:129
  19.4 3.2 %fusion.186 = (bf16[128,1024]{1,0:T(8,128)(2,1)S(1)}, bf16[128,1024]{1,0:T(8,128)(2,1)S(1)}, f32[128,1024]{1,0:T(8,128)S(1)}, f32[128,1024]{1,0:T(8,128)S(1)}) fusion(f32[1024]{0:T(1024)S(1)} %bitcast.228, f32[128]{0:T(128)S(1)} %get-tuple-element.645, f32[1024]{0:T(1024)S(1)} %bitcast.230, f32[128]{0:T(128)S(1)} %get-tuple-element.647, ...), kind=kLoop, calls=%fused_computation.25.clone.1 | loop fusion | flops 3670016 | bytes 2635268 | tf_op jit(solution)/shard_map/convert
  23.7 3.2 %fusion.186 = (bf16[128,1024]{1,0:T(8,128)(2,1)S(1)}, bf16[128,1024]{1,0:T(8,128)(2,1)S(1)}, f32[128,1024]{1,0:T(8,128)S(1)}, f32[128,1024]{1,0:T(8,128)S(1)}) fusion(f32[1024]{0:T(1024)S(1)} %bitcast.228, f32[128]{0:T(128)S(1)} %get-tuple-element.645, f32[1024]{0:T(1024)S(1)} %bitcast.230, f32[128]{0:T(128)S(1)} %get-tuple-element.647, ...), kind=kLoop, calls=%fused_computation.25.clone.1 | loop fusion | flops 3670016 | bytes 2635268 | tf_op jit(solution)/shard_map/convert
  28.0 3.2 %fusion.186 = (bf16[128,1024]{1,0:T(8,128)(2,1)S(1)}, bf16[128,1024]{1,0:T(8,128)(2,1)S(1)}, f32[128,1024]{1,0:T(8,128)S(1)}, f32[128,1024]{1,0:T(8,128)S(1)}) fusion(f32[1024]{0:T(1024)S(1)} %bitcast.228, f32[128]{0:T(128)S(1)} %get-tuple-element.645, f32[1024]{0:T(1024)S(1)} %bitcast.230, f32[128]{0:T(128)S(1)} %get-tuple-element.647, ...), kind=kLoop, calls=%fused_computation.25.clone.1 | loop fusion | flops 3670016 | bytes 2635268 | tf_op jit(solution)/shard_map/convert
  32.3 3.2 %fusion.186 = (bf16[128,1024]{1,0:T(8,128)(2,1)S(1)}, bf16[128,1024]{1,0:T(8,128)(2,1)S(1)}, f32[128,1024]{1,0:T(8,128)S(1)}, f32[128,1024]{1,0:T(8,128)S(1)}) fusion(f32[1024]{0:T(1024)S(1)} %bitcast.228, f32[128]{0:T(128)S(1)} %get-tuple-element.645, f32[1024]{0:T(1024)S(1)} %bitcast.230, f32[128]{0:T(128)S(1)} %get-tuple-element.647, ...), kind=kLoop, calls=%fused_computation.25.clone.1 | loop fusion | flops 3670016 | bytes 2635268 | tf_op jit(solution)/shard_map/convert
  36.6 3.2 %fusion.186 = (bf16[128,1024]{1,0:T(8,128)(2,1)S(1)}, bf16[128,1024]{1,0:T(8,128)(2,1)S(1)}, f32[128,1024]{1,0:T(8,128)S(1)}, f32[128,1024]{1,0:T(8,128)S(1)}) fusion(f32[1024]{0:T(1024)S(1)} %bitcast.228, f32[128]{0:T(128)S(1)} %get-tuple-element.645, f32[1024]{0:T(1024)S(1)} %bitcast.230, f32[128]{0:T(128)S(1)} %get-tuple-element.647, ...), kind=kLoop, calls=%fused_computation.25.clone.1 | loop fusion | flops 3670016 | bytes 2635268 | tf_op jit(solution)/shard_map/convert
  40.9 3.2 %fusion.186 = (bf16[128,1024]{1,0:T(8,128)(2,1)S(1)}, bf16[128,1024]{1,0:T(8,128)(2,1)S(1)}, f32[128,1024]{1,0:T(8,128)S(1)}, f32[128,1024]{1,0:T(8,128)S(1)}) fusion(f32[1024]{0:T(1024)S(1)} %bitcast.228, f32[128]{0:T(128)S(1)} %get-tuple-element.645, f32[1024]{0:T(1024)S(1)} %bitcast.230, f32[128]{0:T(128)S(1)} %get-tuple-element.647, ...), kind=kLoop, calls=%fused_computation.25.clone.1 | loop fusion | flops 3670016 | bytes 2635268 | tf_op jit(solution)/shard_map/convert
  45.2 3.2 %fusion.186 = (bf16[128,1024]{1,0:T(8,128)(2,1)S(1)}, bf16[128,1024]{1,0:T(8,128)(2,1)S(1)}, f32[128,1024]{1,0:T(8,128)S(1)}, f32[128,1024]{1,0:T(8,128)S(1)}) fusion(f32[1024]{0:T(1024)S(1)} %bitcast.228, f32[128]{0:T(128)S(1)} %get-tuple-element.645, f32[1024]{0:T(1024)S(1)} %bitcast.230, f32[128]{0:T(128)S(1)} %get-tuple-element.647, ...), kind=kLoop, calls=%fused_computation.25.clone.1 | loop fusion | flops 3670016 | bytes 2635268 | tf_op jit(solution)/shard_map/convert
  49.5 3.2 %fusion.186 = (bf16[128,1024]{1,0:T(8,128)(2,1)S(1)}, bf16[128,1024]{1,0:T(8,128)(2,1)S(1)}, f32[128,1024]{1,0:T(8,128)S(1)}, f32[128,1024]{1,0:T(8,128)S(1)}) fusion(f32[1024]{0:T(1024)S(1)} %bitcast.228, f32[128]{0:T(128)S(1)} %get-tuple-element.645, f32[1024]{0:T(1024)S(1)} %bitcast.230, f32[128]{0:T(128)S(1)} %get-tuple-element.647, ...), kind=kLoop, calls=%fused_computation.25.clone.1 | loop fusion | flops 3670016 | bytes 2635268 | tf_op jit(solution)/shard_map/convert
  56.0 34.7 %while.46 = (s32[]{:T(128)}, f32[3,1024]{1,0:T(4,128)S(1)}, f32[8,3,128]{2,1,0:T(4,128)S(1)}, f32[8,128,64]{1,2,0:T(8,128)S(1)}, f32[]{:T(128)}, /*index=5*/bf16...) while((s32[]{:T(128)}, f32[3,1024]{1,0:T(4,128)S(1)}, ...), condition=%wide.region_16.17_spmd.clone, body=%wide.region_9.16_spmd.clone.sunk | while | flops 106967936 | bytes 6464403 | solution.py:129
  56.4 3.2 %fusion.197 = (bf16[128,1024]{1,0:T(8,128)(2,1)S(1)}, bf16[128,1024]{1,0:T(8,128)(2,1)S(1)}, f32[128,1024]{1,0:T(8,128)S(1)}, f32[128,1024]{1,0:T(8,128)S(1)}) fusion(f32[1024]{0:T(1024)S(1)} %bitcast.232, f32[128]{0:T(128)S(1)} %get-tuple-element.671, f32[1024]{0:T(1024)S(1)} %bitcast.234, f32[128]{0:T(128)S(1)} %get-tuple-element.673, ...), kind=kLoop, calls=%fused_computation.77.clone.1 | loop fusion | flops 3670016 | bytes 2635268 | tf_op jit(solution)/shard_map/convert.2
  60.8 3.2 %fusion.197 = (bf16[128,1024]{1,0:T(8,128)(2,1)S(1)}, bf16[128,1024]{1,0:T(8,128)(2,1)S(1)}, f32[128,1024]{1,0:T(8,128)S(1)}, f32[128,1024]{1,0:T(8,128)S(1)}) fusion(f32[1024]{0:T(1024)S(1)} %bitcast.232, f32[128]{0:T(128)S(1)} %get-tuple-element.671, f32[1024]{0:T(1024)S(1)} %bitcast.234, f32[128]{0:T(128)S(1)} %get-tuple-element.673, ...), kind=kLoop, calls=%fused_computation.77.clone.1 | loop fusion | flops 3670016 | bytes 2635268 | tf_op jit(solution)/shard_map/convert.2
  65.1 3.2 %fusion.197 = (bf16[128,1024]{1,0:T(8,128)(2,1)S(1)}, bf16[128,1024]{1,0:T(8,128)(2,1)S(1)}, f32[128,1024]{1,0:T(8,128)S(1)}, f32[128,1024]{1,0:T(8,128)S(1)}) fusion(f32[1024]{0:T(1024)S(1)} %bitcast.232, f32[128]{0:T(128)S(1)} %get-tuple-element.671, f32[1024]{0:T(1024)S(1)} %bitcast.234, f32[128]{0:T(128)S(1)} %get-tuple-element.673, ...), kind=kLoop, calls=%fused_computation.77.clone.1 | loop fusion | flops 3670016 | bytes 2635268 | tf_op jit(solution)/shard_map/convert.2
  69.4 3.2 %fusion.197 = (bf16[128,1024]{1,0:T(8,128)(2,1)S(1)}, bf16[128,1024]{1,0:T(8,128)(2,1)S(1)}, f32[128,1024]{1,0:T(8,128)S(1)}, f32[128,1024]{1,0:T(8,128)S(1)}) fusion(f32[1024]{0:T(1024)S(1)} %bitcast.232, f32[128]{0:T(128)S(1)} %get-tuple-element.671, f32[1024]{0:T(1024)S(1)} %bitcast.234, f32[128]{0:T(128)S(1)} %get-tuple-element.673, ...), kind=kLoop, calls=%fused_computation.77.clone.1 | loop fusion | flops 3670016 | bytes 2635268 | tf_op jit(solution)/shard_map/convert.2
  73.8 3.2 %fusion.197 = (bf16[128,1024]{1,0:T(8,128)(2,1)S(1)}, bf16[128,1024]{1,0:T(8,128)(2,1)S(1)}, f32[128,1024]{1,0:T(8,128)S(1)}, f32[128,1024]{1,0:T(8,128)S(1)}) fusion(f32[1024]{0:T(1024)S(1)} %bitcast.232, f32[128]{0:T(128)S(1)} %get-tuple-element.671, f32[1024]{0:T(1024)S(1)} %bitcast.234, f32[128]{0:T(128)S(1)} %get-tuple-element.673, ...), kind=kLoop, calls=%fused_computation.77.clone.1 | loop fusion | flops 3670016 | bytes 2635268 | tf_op jit(solution)/shard_map/convert.2
  78.1 3.2 %fusion.197 = (bf16[128,1024]{1,0:T(8,128)(2,1)S(1)}, bf16[128,1024]{1,0:T(8,128)(2,1)S(1)}, f32[128,1024]{1,0:T(8,128)S(1)}, f32[128,1024]{1,0:T(8,128)S(1)}) fusion(f32[1024]{0:T(1024)S(1)} %bitcast.232, f32[128]{0:T(128)S(1)} %get-tuple-element.671, f32[1024]{0:T(1024)S(1)} %bitcast.234, f32[128]{0:T(128)S(1)} %get-tuple-element.673, ...), kind=kLoop, calls=%fused_computation.77.clone.1 | loop fusion | flops 3670016 | bytes 2635268 | tf_op jit(solution)/shard_map/convert.2
  82.5 3.2 %fusion.197 = (bf16[128,1024]{1,0:T(8,128)(2,1)S(1)}, bf16[128,1024]{1,0:T(8,128)(2,1)S(1)}, f32[128,1024]{1,0:T(8,128)S(1)}, f32[128,1024]{1,0:T(8,128)S(1)}) fusion(f32[1024]{0:T(1024)S(1)} %bitcast.232, f32[128]{0:T(128)S(1)} %get-tuple-element.671, f32[1024]{0:T(1024)S(1)} %bitcast.234, f32[128]{0:T(128)S(1)} %get-tuple-element.673, ...), kind=kLoop, calls=%fused_computation.77.clone.1 | loop fusion | flops 3670016 | bytes 2635268 | tf_op jit(solution)/shard_map/convert.2
  86.8 3.2 %fusion.197 = (bf16[128,1024]{1,0:T(8,128)(2,1)S(1)}, bf16[128,1024]{1,0:T(8,128)(2,1)S(1)}, f32[128,1024]{1,0:T(8,128)S(1)}, f32[128,1024]{1,0:T(8,128)S(1)}) fusion(f32[1024]{0:T(1024)S(1)} %bitcast.232, f32[128]{0:T(128)S(1)} %get-tuple-element.671, f32[1024]{0:T(1024)S(1)} %bitcast.234, f32[128]{0:T(128)S(1)} %get-tuple-element.673, ...), kind=kLoop, calls=%fused_computation.77.clone.1 | loop fusion | flops 3670016 | bytes 2635268 | tf_op jit(solution)/shard_map/convert.2
  92.0 34.4 %while.47 = (s32[]{:T(128)}, f32[3,1024]{1,0:T(4,128)S(1)}, f32[8,3,128]{2,1,0:T(4,128)S(1)}, f32[8,128,64]{1,2,0:T(8,128)S(1)}, f32[]{:T(128)}, /*index=5*/bf16...) while((s32[]{:T(128)}, f32[3,1024]{1,0:T(4,128)S(1)}, ...), condition=%wide.region_24.25_spmd.clone, body=%wide.region_17.24_spmd.clone.sunk | while | flops 106967936 | bytes 6464403 | solution.py:129
  92.4 3.2 %fusion.208 = (bf16[128,1024]{1,0:T(8,128)(2,1)S(1)}, bf16[128,1024]{1,0:T(8,128)(2,1)S(1)}, f32[128,1024]{1,0:T(8,128)S(1)}, f32[128,1024]{1,0:T(8,128)S(1)}) fusion(f32[1024]{0:T(1024)S(1)} %bitcast.236, f32[128]{0:T(128)S(1)} %get-tuple-element.697, f32[1024]{0:T(1024)S(1)} %bitcast.238, f32[128]{0:T(128)S(1)} %get-tuple-element.699, ...), kind=kLoop, calls=%fused_computation.129.clone.1 | loop fusion | flops 3670016 | bytes 2635268 | tf_op jit(solution)/shard_map/convert.4
  96.7 3.2 %fusion.208 = (bf16[128,1024]{1,0:T(8,128)(2,1)S(1)}, bf16[128,1024]{1,0:T(8,128)(2,1)S(1)}, f32[128,1024]{1,0:T(8,128)S(1)}, f32[128,1024]{1,0:T(8,128)S(1)}) fusion(f32[1024]{0:T(1024)S(1)} %bitcast.236, f32[128]{0:T(128)S(1)} %get-tuple-element.697, f32[1024]{0:T(1024)S(1)} %bitcast.238, f32[128]{0:T(128)S(1)} %get-tuple-element.699, ...), kind=kLoop, calls=%fused_computation.129.clone.1 | loop fusion | flops 3670016 | bytes 2635268 | tf_op jit(solution)/shard_map/convert.4
  101.0 3.2 %fusion.208 = (bf16[128,1024]{1,0:T(8,128)(2,1)S(1)}, bf16[128,1024]{1,0:T(8,128)(2,1)S(1)}, f32[128,1024]{1,0:T(8,128)S(1)}, f32[128,1024]{1,0:T(8,128)S(1)}) fusion(f32[1024]{0:T(1024)S(1)} %bitcast.236, f32[128]{0:T(128)S(1)} %get-tuple-element.697, f32[1024]{0:T(1024)S(1)} %bitcast.238, f32[128]{0:T(128)S(1)} %get-tuple-element.699, ...), kind=kLoop, calls=%fused_computation.129.clone.1 | loop fusion | flops 3670016 | bytes 2635268 | tf_op jit(solution)/shard_map/convert.4
  105.3 3.2 %fusion.208 = (bf16[128,1024]{1,0:T(8,128)(2,1)S(1)}, bf16[128,1024]{1,0:T(8,128)(2,1)S(1)}, f32[128,1024]{1,0:T(8,128)S(1)}, f32[128,1024]{1,0:T(8,128)S(1)}) fusion(f32[1024]{0:T(1024)S(1)} %bitcast.236, f32[128]{0:T(128)S(1)} %get-tuple-element.697, f32[1024]{0:T(1024)S(1)} %bitcast.238, f32[128]{0:T(128)S(1)} %get-tuple-element.699, ...), kind=kLoop, calls=%fused_computation.129.clone.1 | loop fusion | flops 3670016 | bytes 2635268 | tf_op jit(solution)/shard_map/convert.4
  138.7 19.7 %reduce-scatter.4.cloned.1.call-done = f32[256,3]{1,0:T(8,128)} async-done(((f32[1024,3]{1,0:T(8,128)}), f32[256,3]{1,0:T(8,128)}) %reduce-scatter.4.cloned.1.call-update) | async-done | bytes 3088
  (260 shorter events, 67.8 us)
Async XLA Ops:
  7.2 151.2 %reduce-scatter.4.cloned.1.call-start = ((), (), s32[]{:S(2)}) async-start(), calls=%async_computation.1 | async-start | bytes 655360
  7.2 46.3 %collective-permute-start.1 = (bf16[1024,128]{1,0:T(8,128)(2,1)}, bf16[1024,128]{1,0:T(8,128)(2,1)S(1)}, u32[]{:S(2)}, u32[]{:S(2)}) collective-permute-start(bf16[1024,128]{1,0:T(8,128)(2,1)} %bitcast.219), channel_id=1, source_target_pairs={{0,4},{4,8},{8,12},{12,0},{1,5},{5,9},{9,13},{13,1},{2,6},{6,10},{... | collective-permute-start | bytes 786440 | tf_op jit(solution)/shard_map/ppermute | solution.py:29
  10.3 8.7 %collective-permute-start = (bf16[3,1024]{1,0:T(4,128)(2,1)}, bf16[3,1024]{1,0:T(4,128)(2,1)S(1)}, u32[]{:S(2)}, u32[]{:S(2)}) collective-permute-start(bf16[3,1024]{1,0:T(4,128)(2,1)} %param.10), channel_id=1, source_target_pairs={{0,4},{4,8},{8,12},{12,0},{1,5},{5,9},{9,13},{13,1},{2,6},{6,10},{... | collective-permute-start | bytes 18440 | tf_op jit(solution)/shard_map/ppermute | solution.py:29
  11.9 1.7 %copy-start = (bf16[1,1024,128]{2,1,0:T(8,128)(2,1)S(1)}, bf16[1,1024,128]{2,1,0:T(8,128)(2,1)}, u32[]{:S(2)}) copy-start(bf16[1,1024,128]{2,1,0:T(8,128)(2,1)} %param.11) | copy-start | bytes 786436
  13.7 0.7 copy-start.2
  13.7 0.7 copy-start.3
  14.8 1.2 copy-start.1
  19.0 34.5 %collective-permute-start.2 = (bf16[3,1024]{1,0:T(4,128)(2,1)S(1)}, bf16[3,1024]{1,0:T(4,128)(2,1)S(1)}, u32[]{:S(2)}, u32[]{:S(2)}) collective-permute-start(bf16[3,1024]{1,0:T(4,128)(2,1)S(1)} %collective-permute-done), channel_id=1, source_target_pairs={{0,4},{4,8},{8,12},{12,0},{1,5},{5,9},{9,13},{13,1},{2,6},{6,10},{... | collective-permute-start | bytes 18440 | tf_op jit(solution)/shard_map/ppermute | solution.py:29
  54.7 36.1 %collective-permute-start.3 = (bf16[1024,128]{1,0:T(8,128)(2,1)S(1)}, bf16[1024,128]{1,0:T(8,128)(2,1)S(1)}, u32[]{:S(2)}, u32[]{:S(2)}) collective-permute-start(bf16[1024,128]{1,0:T(8,128)(2,1)S(1)} %collective-permute-done.1), channel_id=1, source_target_pairs={{0,4},{4,8},{8,12},{12,0},{1,5},{5,9},{9,13},{13,1},{2,6},{6,10},{... | collective-permute-start | bytes 786440 | tf_op jit(solution)/shard_map/ppermute | solution.py:29
  127.6 4.6 %collective-permute-start.6 = (f32[2,32,32]{1,2,0:T(8,128)S(1)}, f32[2,32,32]{1,2,0:T(8,128)S(1)}, u32[]{:S(2)}, u32[]{:S(2)}) collective-permute-start(f32[2,32,32]{1,2,0:T(8,128)S(1)} %pad_maximum_fusion), channel_id=1, source_target_pairs={{0,4},{4,0},{8,12},{12,8},{1,5},{5,1},{9,13},{13,9},{2,6},{6,2},{1... | collective-permute-start | bytes 24584 | tf_op jit(solution)/shard_map/ppermute | solution.py:18
  129.3 6.0 %collective-permute-start.4 = (f32[3,1024]{1,0:T(4,128)S(1)}, f32[3,1024]{1,0:T(4,128)S(1)}, u32[]{:S(2)}, u32[]{:S(2)}) collective-permute-start(f32[3,1024]{1,0:T(4,128)S(1)} %get-tuple-element.168), channel_id=1, source_target_pairs={{0,12},{4,0},{8,4},{12,8},{1,13},{5,1},{9,5},{13,9},{2,14},{6,2},{... | collective-permute-start | bytes 36872 | tf_op jit(solution)/shard_map/ppermute | solution.py:29
  132.2 4.6 %collective-permute-start.5 = (f32[3,1024]{1,0:T(4,128)S(1)}, f32[3,1024]{1,0:T(4,128)S(1)}, u32[]{:S(2)}, u32[]{:S(2)}) collective-permute-start(f32[3,1024]{1,0:T(4,128)S(1)} %get-tuple-element.169), channel_id=1, source_target_pairs={{0,8},{4,12},{8,0},{12,4},{1,9},{5,13},{9,1},{13,5},{2,10},{6,14},... | collective-permute-start | bytes 36872 | tf_op jit(solution)/shard_map/ppermute | solution.py:29
  132.3 5.7 %collective-permute-start.7 = (f32[2,32,32]{1,2,0:T(8,128)S(1)}, f32[2,32,32]{1,2,0:T(8,128)S(1)}, u32[]{:S(2)}, u32[]{:S(2)}) collective-permute-start(f32[2,32,32]{1,2,0:T(8,128)S(1)} %fusion.125), channel_id=1, source_target_pairs={{0,8},{4,12},{8,0},{12,4},{1,9},{5,13},{9,1},{13,5},{2,10},{6,14},... | collective-permute-start | bytes 24584 | tf_op jit(solution)/shard_map/ppermute | solution.py:18
Sparse Core Ops, SparseCore 0:
  138.1 20.2 reduce-scatter.3
